TPU v7x, 256 devices: a whole 4x4x8 slice. The times are simulated.
256 devices in a mesh: seq: 64 (over z, x, y_lo), sub: 4 (over y_hi, core).
Axes of the slice: x: 4, y: 4 (y_hi: 2, y_lo: 2; y = y_hi * 2 + y_lo), z: 8, core: 2. Of those that a mesh axis runs over, the one named last changes fastest.
Arguments:
- features: bfloat16 [262144, 768], P(('seq', 'sub')), may hold values from -6 to 6
- kernel: bfloat16 [3, 768, 384], replicated, may hold values from -0.125 to 0.125
- offsets: float32 [384], replicated, may hold values from -3 to 3
- mixer: bfloat16 [384, 768], replicated, may hold values from -0.3125 to 0.3125
- biases: float32 [768], replicated, may hold values from -3 to 3
- cotangent: bfloat16 [262144, 768], P(('seq', 'sub')), may hold values from -6 to 6
Outputs:
- layer_output: bfloat16 [262144, 768], P(('seq', 'sub'))
- input_grad: bfloat16 [262144, 768], P(('seq', 'sub'))
- kernel_grad: float32 [3, 768, 384], replicated
- offset_grad: float32 [384], replicated
- mixer_grad: float32 [384, 768], replicated
- biases_grad: float32 [768], replicated
All inputs are finite; a program needn't handle non-finite values.
Results may differ from a plain program's by a relative error of at most 0.0075.
Values may be sent and summed in bfloat16 or wider, within the bound.
A program may use at most 64 MiB of HBM per device.

v0:
```python
import math
import jax
import jax.numpy as jnp
from jax import lax
from jax.sharding import PartitionSpec as P

DILATION_STEP = 8192


def from_behind(value, axis, steps):
    count = lax.axis_size(axis)
    pairs = [(source, (source + steps) % count) for source in range(count)]
    return lax.ppermute(value, axis, pairs)


def gelu_exact(values):
    return jax.nn.gelu(values, approximate=False)


def gelu_slope(values):
    normal_cdf = 0.5 * (1.0 + jax.scipy.special.erf(values / math.sqrt(2.0)))
    return normal_cdf + values * jnp.exp(-0.5 * values * values) / math.sqrt(2.0 * math.pi)


def contract_rows(left, right):
    return lax.dot_general(
        left, right, (((0,), (0,)), ((), ())), preferred_element_type=jnp.float32
    )


def times_transposed(left, right):
    return lax.dot_general(
        left, right, (((1,), (1,)), ((), ())), preferred_element_type=jnp.float32
    )


def local(features, kernel, offsets, mixer, biases, cotangent):
    partition_rows = features.shape[0]
    offset_distance = DILATION_STEP // (partition_rows * lax.axis_size("sub"))
    factor = 1.0 / math.sqrt(partition_rows * lax.axis_size("seq") * lax.axis_size("sub"))
    inputs = features.astype(jnp.float32)
    activated_output = gelu_exact(inputs).astype(jnp.bfloat16)
    send_early = jnp.dot(activated_output, kernel[0], preferred_element_type=jnp.float32).astype(
        jnp.bfloat16
    )
    send_late = jnp.dot(activated_output, kernel[2], preferred_element_type=jnp.float32).astype(
        jnp.bfloat16
    )
    tap_early = from_behind(send_early, "seq", offset_distance)
    tap_late = from_behind(send_late, "seq", -offset_distance)
    preact = (
        jnp.dot(activated_output, kernel[1], preferred_element_type=jnp.float32)
        + tap_early.astype(jnp.float32)
        + tap_late.astype(jnp.float32)
        + offsets
    )
    hidden = gelu_exact(preact).astype(jnp.bfloat16)
    layer_output = (
        inputs + jnp.dot(hidden, mixer, preferred_element_type=jnp.float32) + biases
    ).astype(jnp.bfloat16)
    cot_float = cotangent.astype(jnp.float32)
    mixer_part = contract_rows(hidden, cotangent) * factor
    biases_part = jnp.sum(cot_float, axis=0) * factor
    hidden_grad = times_transposed(cotangent, mixer)
    preactivation_grad = (hidden_grad * gelu_slope(preact)).astype(jnp.bfloat16)
    grad_later = from_behind(preactivation_grad, "seq", -offset_distance)
    grad_earlier = from_behind(preactivation_grad, "seq", offset_distance)
    kernel_part = (
        jnp.stack(
            [
                contract_rows(activated_output, grad_later),
                contract_rows(activated_output, preactivation_grad),
                contract_rows(activated_output, grad_earlier),
            ]
        )
        * factor
    )
    offset_part = jnp.sum(preactivation_grad.astype(jnp.float32), axis=0) * factor
    activated_output_grad = (
        times_transposed(preactivation_grad, kernel[1])
        + times_transposed(grad_later, kernel[0])
        + times_transposed(grad_earlier, kernel[2])
    )
    input_grad = (cot_float + activated_output_grad * gelu_slope(inputs)).astype(jnp.bfloat16)
    kernel_grad, offset_grad, mixer_grad, biases_grad = lax.psum(
        (kernel_part, offset_part, mixer_part, biases_part), ("seq", "sub")
    )
    return (layer_output, input_grad, kernel_grad, offset_grad, mixer_grad, biases_grad)


def solution(mesh):
    placed = (P(("seq", "sub"), None), P(), P(), P(), P(), P(("seq", "sub"), None))
    return jax.shard_map(
        local,
        mesh=mesh,
        in_specs=placed,
        out_specs=(P(("seq", "sub"), None), P(("seq", "sub"), None), P(), P(), P(), P()),
        check_vma=False,
    )
```

profile of v0, /device:TPU:2, one launch (start us, length us, event | category | flops | bytes accessed | tf_op | source)
XLA Modules:
  0.0 358.5 jit_solution(11011791587891050671)
XLA Ops:
  7.2 0.0 copy-start
  7.2 0.0 all-reduce.4.cloned.1.call-start
  7.2 0.0 copy-start.4
  7.2 8.0 %fusion.3 = bf16[1024,768]{1,0:T(8,128)(2,1)S(1)} fusion(bf16[1024,768]{1,0:T(8,128)(2,1)} %param.6), kind=kLoop, calls=%fused_computation.14 | loop fusion | flops 51904512 | bytes 3145728 | tf_op jit(solution)/shard_map/convert_element_type | solution.py:42
  15.3 1.0 convolution_convert_fusion.1
  16.3 1.6 collective-permute-start
  17.9 1.0 convolution_convert_fusion
  18.8 0.9 collective-permute-start.1
  19.7 15.9 %collective-permute-done = bf16[1024,384]{1,0:T(8,128)(2,1)S(1)} collective-permute-done((bf16[1024,384]{1,0:T(8,128)(2,1)S(1)}, bf16[1024,384]{1,0:T(8,128)(2,1)S(1)}, u32[]{:S(2)}, u32[]{:S(2)}) %collective-permute-start) | collective-permute-done | bytes 786464 | tf_op jit(solution)/shard_map/ppermute | solution.py:13
  35.6 2.3 collective-permute-done.1
  37.9 4.3 %fusion.43 = (bf16[1024,384]{1,0:T(8,128)(2,1)S(1)}, f32[1024,384]{1,0:T(8,128)S(1)}) fusion(f32[384]{0:T(512)S(1)} %copy-done.12, bf16[1024,384]{1,0:T(8,128)(2,1)S(1)} %collective-permute-done.1, bf16[1024,384]{1,0:T(8,128)(2,1)S(1)} %collective-permute-done, bf16[1024,768]{1,0:T(8,128)(2,1)S(1)} %fusion.3, bf16[3,768,384]{2,1,0:T(8,128)(2,1)S(1)} %copy-done.4), kind=kOutput, calls=%fused_computation.56 | convolution fusion | flops 631504896 | bytes 6096896 | tf_op jit(solution)/shard_map/dot_general | solution.py:52
  42.3 1.3 convert_reduce_fusion.1
  43.6 1.4 collective-permute-start.3
  45.0 3.9 %collective-permute-start.2 = (bf16[1024,384]{1,0:T(8,128)(2,1)S(1)}, bf16[1024,384]{1,0:T(8,128)(2,1)S(1)}, u32[]{:S(2)}, u32[]{:S(2)}) collective-permute-start(bf16[1024,384]{1,0:T(8,128)(2,1)S(1)} %get-tuple-element.13), channel_id=1, source_target_pairs={{0,248},{4,252},{8,0},{12,4},{16,8},{20,12},{24,16},{28,20},{32,24... | collective-permute-start | bytes 2359304 | tf_op jit(solution)/shard_map/ppermute | solution.py:13
  48.9 1.0 convolution_bitcast_fusion.1
  49.9 1.8 convolution_multiply_fusion
  51.7 13.6 %collective-permute-done.3 = bf16[1024,384]{1,0:T(8,128)(2,1)S(1)} collective-permute-done((bf16[1024,384]{1,0:T(8,128)(2,1)S(1)}, bf16[1024,384]{1,0:T(8,128)(2,1)S(1)}, u32[]{:S(2)}, u32[]{:S(2)}) %collective-permute-start.3) | collective-permute-done | bytes 786464 | tf_op jit(solution)/shard_map/ppermute | solution.py:13
  65.3 1.0 convolution_bitcast_fusion
  66.3 0.9 copy-done.7
  67.2 1.0 convolution_bitcast_fusion.2
  68.2 2.0 maximum_multiply_fusion
  70.2 0.0 all-reduce.4.cloned.1.call-update
  70.3 0.3 convert_reduce_fusion
  70.6 80.6 %all-reduce = (f32[384]{0:T(512)}, f32[768]{0:T(1024)}) all-reduce(f32[384]{0:T(512)S(1)} %broadcast_multiply_fusion.1, f32[768]{0:T(1024)S(1)} %broadcast_multiply_fusion), channel_id=1, replica_groups=mesh['seq'=64,'sub'=4] {'seq','sub'}, use_global_device_ids=true, to_apply=%region_2.0 | all-reduce | flops 1152 | bytes 9216 | tf_op jit(solution)/shard_map/psum | solution.py:85
  151.2 2.4 fusion.62
  153.6 2.1 fusion.33
  155.8 1.0 fusion.59
  156.8 0.1 copy-done.10
  156.9 3.4 fusion
  160.4 186.1 %all-reduce.4.cloned.1.call-done = (f32[3,768,384]{2,1,0:T(8,128)}, f32[384,768]{1,0:T(8,128)}) async-done(((f32[3,768,384]{2,1,0:T(8,128)}, f32[384,768]{1,0:T(8,128)}), (f32[3,768,384]{2,1,0:T(8,128)}, f32[384,768]{1,0:T(8,128)})) %all-reduce.4.cloned.1.call-update) | async-done | bytes 4718608 | tf_op jit(solution)/shard_map/psum | solution.py:85
  346.5 4.1 %copy.14 = f32[3,768,384]{2,1,0:T(8,128)} copy(f32[3,768,384]{2,1,0:T(8,128)} %get-tuple-element.16) | data formatting | bytes 7077888
  350.6 1.0 copy.15
  (25 shorter events, 0.1 us)
Async XLA Ops:
  7.2 35.1 %copy-start = (bf16[384,768]{1,0:T(8,128)(2,1)S(1)}, bf16[384,768]{1,0:T(8,128)(2,1)}, u32[]{:S(2)}) copy-start(bf16[384,768]{1,0:T(8,128)(2,1)} %param.9) | copy-start | bytes 1769476
  7.2 339.3 %all-reduce.4.cloned.1.call-start = ((), (), s32[]{:S(2)}) async-start(), calls=%async_computation | async-start | bytes 9437184 | tf_op jit(solution)/shard_map/psum | solution.py:85
  7.2 8.1 %copy-start.4 = (bf16[3,768,384]{2,1,0:T(8,128)(2,1)S(1)}, bf16[3,768,384]{2,1,0:T(8,128)(2,1)}, u32[]{:S(2)}) copy-start(bf16[3,768,384]{2,1,0:T(8,128)(2,1)} %param.7) | copy-start | bytes 5308420
  16.3 21.7 %copy-start.12 = (f32[384]{0:T(512)S(1)}, f32[384]{0:T(512)}, u32[]{:S(2)}) copy-start(f32[384]{0:T(512)} %param.8) | copy-start | bytes 4612
  16.3 19.4 %collective-permute-start = (bf16[1024,384]{1,0:T(8,128)(2,1)S(1)}, bf16[1024,384]{1,0:T(8,128)(2,1)S(1)}, u32[]{:S(2)}, u32[]{:S(2)}) collective-permute-start(bf16[1024,384]{1,0:T(8,128)(2,1)S(1)} %convolution_convert_fusion.1), channel_id=1, source_target_pairs={{0,8},{4,12},{8,16},{12,20},{16,24},{20,28},{24,32},{28,36},{32,40... | collective-permute-start | bytes 2359304 | tf_op jit(solution)/shard_map/ppermute | solution.py:13
  18.8 23.4 %copy-start.1 = (bf16[1024,768]{1,0:T(8,128)(2,1)S(1)}, bf16[1024,768]{1,0:T(8,128)(2,1)}, u32[]{:S(2)}) copy-start(bf16[1024,768]{1,0:T(8,128)(2,1)} %param.11) | copy-start | bytes 4718596
  18.8 19.1 %collective-permute-start.1 = (bf16[1024,384]{1,0:T(8,128)(2,1)S(1)}, bf16[1024,384]{1,0:T(8,128)(2,1)S(1)}, u32[]{:S(2)}, u32[]{:S(2)}) collective-permute-start(bf16[1024,384]{1,0:T(8,128)(2,1)S(1)} %convolution_convert_fusion), channel_id=1, source_target_pairs={{0,248},{4,252},{8,0},{12,4},{16,8},{20,12},{24,16},{28,20},{32,24... | collective-permute-start | bytes 2359304 | tf_op jit(solution)/shard_map/ppermute | solution.py:13
  43.6 6.3 %copy-start.6 = (bf16[1024,384]{1,0:T(8,128)(2,1)}, bf16[1024,384]{1,0:T(8,128)(2,1)S(1)}, u32[]{:S(2)}) copy-start(bf16[1024,384]{1,0:T(8,128)(2,1)S(1)} %get-tuple-element.13) | copy-start | bytes 2359300
  43.6 21.6 %collective-permute-start.3 = (bf16[1024,384]{1,0:T(8,128)(2,1)S(1)}, bf16[1024,384]{1,0:T(8,128)(2,1)S(1)}, u32[]{:S(2)}, u32[]{:S(2)}) collective-permute-start(bf16[1024,384]{1,0:T(8,128)(2,1)S(1)} %get-tuple-element.13), channel_id=1, source_target_pairs={{0,8},{4,12},{8,16},{12,20},{16,24},{20,28},{24,32},{28,36},{32,40... | collective-permute-start | bytes 2359304 | tf_op jit(solution)/shard_map/ppermute | solution.py:13
  45.0 21.3 %collective-permute-start.2 = (bf16[1024,384]{1,0:T(8,128)(2,1)S(1)}, bf16[1024,384]{1,0:T(8,128)(2,1)S(1)}, u32[]{:S(2)}, u32[]{:S(2)}) collective-permute-start(bf16[1024,384]{1,0:T(8,128)(2,1)S(1)} %get-tuple-element.13), channel_id=1, source_target_pairs={{0,248},{4,252},{8,0},{12,4},{16,8},{20,12},{24,16},{28,20},{32,24... | collective-permute-start | bytes 2359304 | tf_op jit(solution)/shard_map/ppermute | solution.py:13
  65.3 1.0 copy-start.9
  66.3 0.9 copy-start.7
  151.2 2.4 copy-start.2
  151.2 2.4 copy-start.11
  153.6 2.1 copy-start.5
  153.6 2.1 copy-start.8
  155.8 1.1 copy-start.10
  346.5 4.1 %copy-start.3 = (f32[384,768]{1,0:T(8,128)S(1)}, f32[384,768]{1,0:T(8,128)}, u32[]{:S(2)}) copy-start(f32[384,768]{1,0:T(8,128)} %get-tuple-element.18) | copy-start | bytes 3538948
Sparse Core Ops, SparseCore 0:
  70.4 276.0 all-reduce.3
where the time goes:
time: 359 us; the launch traced here: 358 us
  waiting for transfers between devices  218 us (61%)
  blocking collectives  80.6 us (22%)
  matrix products  21.5 us (6%)
  between operations  14.2 us (4%)
  other arithmetic  10.4 us (3%)
  starting transfers between devices  7.73 us (2%)
  local copies, waits for them, and re-layouts  6.19 us (2%)
    psum x1, waiting for transfers between devices, local(): lax.psum((kernel_part, offset_part, mixer_part, biases_part), ('seq', 'su...  186 us
    psum x1, blocking collectives, local(): lax.psum((kernel_part, offset_part, mixer_part, biases_part), ('seq', 'su...  80.6 us
    ppermute x4, waiting for transfers between devices, from_behind(): return lax.ppermute(value, axis, pairs)  31.8 us
    dot_general x4, matrix products, times_transposed(): lax.dot_general(left, right, (((1,), (1,)), ((), ())), preferred_element_...  8.22 us
    convert_element_type x1, other arithmetic, local(): activated_output = gelu_exact(inputs).astype(jnp.bfloat16)  8.04 us
    ppermute x4, starting transfers between devices, from_behind(): return lax.ppermute(value, axis, pairs)  7.69 us
  transfers between devices with their start and end apart: 5, of which 4 were waited for; matrix products, arithmetic and copies ran while one was open for 4% of the time, Pallas kernels for 0%

commit v1 on v0

--- a/solution.py
+++ b/solution.py
@@ -35,6 +35,12 @@
 
 
 def local(features, kernel, offsets, mixer, biases, cotangent):
+
+    def hubs_set(in_array):
+        moved = lax.psum(in_array, axis_name="sub")
+        u_next = lax.psum(moved, axis_name="seq")
+        return u_next
+
     partition_rows = features.shape[0]
     offset_distance = DILATION_STEP // (partition_rows * lax.axis_size("sub"))
     factor = 1.0 / math.sqrt(partition_rows * lax.axis_size("seq") * lax.axis_size("sub"))
@@ -82,8 +88,8 @@
         + times_transposed(grad_earlier, kernel[2])
     )
     input_grad = (cot_float + activated_output_grad * gelu_slope(inputs)).astype(jnp.bfloat16)
-    kernel_grad, offset_grad, mixer_grad, biases_grad = lax.psum(
-        (kernel_part, offset_part, mixer_part, biases_part), ("seq", "sub")
+    kernel_grad, offset_grad, mixer_grad, biases_grad = hubs_set(
+        (kernel_part, offset_part, mixer_part, biases_part)
     )
     return (layer_output, input_grad, kernel_grad, offset_grad, mixer_grad, biases_grad)
 

time: 359 us -> 819 us (2.28)
  waiting for transfers between devices: 218 us -> 593 us
  blocking collectives: 80.6 us -> 166 us
    psum x1 -> x2, waiting for transfers between devices: 186 us -> 562 us  [the longest x1 451 us: hubs_set(): u_next = lax.psum(moved, axis_name='seq')]
    psum x1 -> x2, blocking collectives: 80.6 us -> 166 us  [the longest x1 158 us: hubs_set(): u_next = lax.psum(moved, axis_name='seq')]
  transfers between devices with their start and end apart: 5 -> 6, of which waited for: 4 -> 5; matrix products, arithmetic and copies ran while one was open for 4% -> 2% of each run, Pallas kernels for 0% -> 0%
where the time goes in v1:
time: 819 us
  waiting for transfers between devices  593 us (72%)
  blocking collectives  166 us (20%)
  matrix products  21.5 us (3%)
  between operations  14.2 us (2%)
  other arithmetic  10.4 us (1%)
    psum x1, waiting for transfers between devices, hubs_set(): u_next = lax.psum(moved, axis_name='seq')  451 us
    psum x1, blocking collectives, hubs_set(): u_next = lax.psum(moved, axis_name='seq')  158 us
    psum x1, waiting for transfers between devices, hubs_set(): moved = lax.psum(in_array, axis_name='sub')  111 us
    ppermute x4, waiting for transfers between devices, from_behind(): return lax.ppermute(value, axis, pairs)  31.8 us
  transfers between devices with their start and end apart: 6, of which 5 were waited for; matrix products, arithmetic and copies ran while one was open for 2% of the time, Pallas kernels for 0%

profile of v1, /device:TPU:2, one launch (start us, length us, event | category | flops | bytes accessed | tf_op | source)
XLA Modules:
  0.0 819.1 jit_solution(146481156764189459)
XLA Ops:
  7.2 0.0 all-reduce.9.cloned.1.call-start
  7.2 8.0 fusion.3
  15.3 1.0 convolution_convert_fusion.1
  16.3 1.6 collective-permute-start
  17.9 1.0 convolution_convert_fusion
  18.8 0.9 collective-permute-start.1
  19.7 15.9 %collective-permute-done = bf16[1024,384]{1,0:T(8,128)(2,1)S(1)} collective-permute-done((bf16[1024,384]{1,0:T(8,128)(2,1)S(1)}, bf16[1024,384]{1,0:T(8,128)(2,1)S(1)}, u32[]{:S(2)}, u32[]{:S(2)}) %collective-permute-start) | collective-permute-done | bytes 786464 | tf_op jit(solution)/shard_map/ppermute | solution.py:13
  35.6 2.3 collective-permute-done.1
  37.9 4.3 fusion.43
  42.3 1.3 convert_reduce_fusion.1
  43.6 1.4 collective-permute-start.3
  45.0 3.9 collective-permute-start.2
  48.9 1.0 convolution_bitcast_fusion.1
  49.9 1.8 convolution_multiply_fusion
  51.7 13.6 %collective-permute-done.3 = bf16[1024,384]{1,0:T(8,128)(2,1)S(1)} collective-permute-done((bf16[1024,384]{1,0:T(8,128)(2,1)S(1)}, bf16[1024,384]{1,0:T(8,128)(2,1)S(1)}, u32[]{:S(2)}, u32[]{:S(2)}) %collective-permute-start.3) | collective-permute-done | bytes 786464 | tf_op jit(solution)/shard_map/ppermute | solution.py:13
  65.3 1.0 convolution_bitcast_fusion
  66.3 0.9 copy-done.7
  67.2 1.0 convolution_bitcast_fusion.2
  68.2 2.0 maximum_multiply_fusion
  70.3 0.0 all-reduce.7.cloned.1.call-start
  70.3 110.9 %all-reduce.9.cloned.1.call-done = (f32[3,768,384]{2,1,0:T(8,128)}, f32[384,768]{1,0:T(8,128)}) async-done(((f32[3,768,384]{2,1,0:T(8,128)}, f32[384,768]{1,0:T(8,128)}), (f32[3,768,384]{2,1,0:T(8,128)}, f32[384,768]{1,0:T(8,128)})) %all-reduce.9.cloned.1.call-update) | async-done | bytes 4718608 | tf_op jit(solution)/shard_map/psum | solution.py:40
  181.3 0.3 convert_reduce_fusion
  181.6 7.6 all-reduce.2
  189.2 157.9 %all-reduce = (f32[384]{0:T(512)}, f32[768]{0:T(1024)}) all-reduce(f32[384]{0:T(512)S(1)} %get-tuple-element.10, f32[768]{0:T(1024)S(1)} %get-tuple-element.11), channel_id=1, replica_groups=mesh['seq'=64,'sub'=4] {'seq'}, use_global_device_ids=true, to_apply=%region_4.0 | all-reduce | flops 1152 | bytes 9216 | tf_op jit(solution)/shard_map/psum | solution.py:41
  347.1 2.4 fusion.62
  349.6 2.1 fusion.33
  351.7 1.0 fusion.59
  352.7 0.1 copy-done.10
  352.9 3.4 fusion
  356.3 450.8 %all-reduce.7.cloned.1.call-done = (f32[3,768,384]{2,1,0:T(8,128)}, f32[384,768]{1,0:T(8,128)}) async-done(((f32[3,768,384]{2,1,0:T(8,128)}, f32[384,768]{1,0:T(8,128)}), (f32[3,768,384]{2,1,0:T(8,128)}, f32[384,768]{1,0:T(8,128)})) %all-reduce.7.cloned.1.call-update) | async-done | bytes 4718608 | tf_op jit(solution)/shard_map/psum | solution.py:41
  807.1 4.1 copy.16
  811.2 1.0 copy.17
  (29 shorter events, 0.1 us)
Async XLA Ops:
  7.2 35.1 %copy-start = (bf16[384,768]{1,0:T(8,128)(2,1)S(1)}, bf16[384,768]{1,0:T(8,128)(2,1)}, u32[]{:S(2)}) copy-start(bf16[384,768]{1,0:T(8,128)(2,1)} %param.9) | copy-start | bytes 1769476
  7.2 174.1 %all-reduce.9.cloned.1.call-start = ((), (), s32[]{:S(2)}) async-start(), calls=%async_computation.1 | async-start | bytes 9437184 | tf_op jit(solution)/shard_map/psum | solution.py:40
  7.2 8.1 copy-start.4
  16.3 21.7 %copy-start.12 = (f32[384]{0:T(512)S(1)}, f32[384]{0:T(512)}, u32[]{:S(2)}) copy-start(f32[384]{0:T(512)} %param.8) | copy-start | bytes 4612
  16.3 19.4 %collective-permute-start = (bf16[1024,384]{1,0:T(8,128)(2,1)S(1)}, bf16[1024,384]{1,0:T(8,128)(2,1)S(1)}, u32[]{:S(2)}, u32[]{:S(2)}) collective-permute-start(bf16[1024,384]{1,0:T(8,128)(2,1)S(1)} %convolution_convert_fusion.1), channel_id=1, source_target_pairs={{0,8},{4,12},{8,16},{12,20},{16,24},{20,28},{24,32},{28,36},{32,40... | collective-permute-start | bytes 2359304 | tf_op jit(solution)/shard_map/ppermute | solution.py:13
  18.8 23.4 %copy-start.1 = (bf16[1024,768]{1,0:T(8,128)(2,1)S(1)}, bf16[1024,768]{1,0:T(8,128)(2,1)}, u32[]{:S(2)}) copy-start(bf16[1024,768]{1,0:T(8,128)(2,1)} %param.11) | copy-start | bytes 4718596
  18.8 19.1 %collective-permute-start.1 = (bf16[1024,384]{1,0:T(8,128)(2,1)S(1)}, bf16[1024,384]{1,0:T(8,128)(2,1)S(1)}, u32[]{:S(2)}, u32[]{:S(2)}) collective-permute-start(bf16[1024,384]{1,0:T(8,128)(2,1)S(1)} %convolution_convert_fusion), channel_id=1, source_target_pairs={{0,248},{4,252},{8,0},{12,4},{16,8},{20,12},{24,16},{28,20},{32,24... | collective-permute-start | bytes 2359304 | tf_op jit(solution)/shard_map/ppermute | solution.py:13
  43.6 6.3 copy-start.6
  43.6 21.6 %collective-permute-start.3 = (bf16[1024,384]{1,0:T(8,128)(2,1)S(1)}, bf16[1024,384]{1,0:T(8,128)(2,1)S(1)}, u32[]{:S(2)}, u32[]{:S(2)}) collective-permute-start(bf16[1024,384]{1,0:T(8,128)(2,1)S(1)} %get-tuple-element.17), channel_id=1, source_target_pairs={{0,8},{4,12},{8,16},{12,20},{16,24},{20,28},{24,32},{28,36},{32,40... | collective-permute-start | bytes 2359304 | tf_op jit(solution)/shard_map/ppermute | solution.py:13
  45.0 21.3 %collective-permute-start.2 = (bf16[1024,384]{1,0:T(8,128)(2,1)S(1)}, bf16[1024,384]{1,0:T(8,128)(2,1)S(1)}, u32[]{:S(2)}, u32[]{:S(2)}) collective-permute-start(bf16[1024,384]{1,0:T(8,128)(2,1)S(1)} %get-tuple-element.17), channel_id=1, source_target_pairs={{0,248},{4,252},{8,0},{12,4},{16,8},{20,12},{24,16},{28,20},{32,24... | collective-permute-start | bytes 2359304 | tf_op jit(solution)/shard_map/ppermute | solution.py:13
  65.3 1.0 copy-start.9
  66.3 0.9 copy-start.7
  70.3 736.8 %all-reduce.7.cloned.1.call-start = ((), (), s32[]{:S(2)}) async-start(), calls=%async_computation | async-start | bytes 9437184 | tf_op jit(solution)/shard_map/psum | solution.py:41
  347.1 2.4 copy-start.2
  347.1 2.4 copy-start.11
  349.6 2.1 copy-start.5
  349.6 2.1 copy-start.8
  351.7 1.1 copy-start.10
  807.1 4.1 copy-start.3
Sparse Core Ops, SparseCore 0:
  70.4 110.8 all-reduce.8
  184.0 623.0 all-reduce.6
